TPU v7x, 32 devices: a whole 2x2x4 slice. The times are simulated.
32 devices in a mesh: dp: 8 (over z, core), tensor: 4 (over y, x).
Axes of the slice: x: 2, y: 2, z: 4, core: 2. Of those that a mesh axis runs over, the one named last changes fastest.
Arguments:
- block_input: bfloat16 [8192, 2048], P('dp'), may hold values from -6 to 6
- block_owner: int32 [64], P('dp'), may hold values from 0 to 63, as said below
- token_mask: int32 [8192], P('dp'), may hold values from 0 to 1, as said below
- attention_gain: float32 [2048], replicated, may hold values from 0.5 to 1.5
- query_weight: bfloat16 [2048, 2048], P(None, 'tensor')
- key_weight: bfloat16 [2048, 2048], P(None, 'tensor')
- value_weight: bfloat16 [2048, 2048], P(None, 'tensor'), may hold values from -0.125 to 0.125
- output_weight: bfloat16 [2048, 2048], P('tensor'), may hold values from -0.5 to 0.5
- feedforward_gain: float32 [2048], replicated, may hold values from 0.5 to 1.5
- gate_weight: bfloat16 [2048, 8192], P(None, 'tensor'), may hold values from -0.125 to 0.125
- up_weight: bfloat16 [2048, 8192], P(None, 'tensor'), may hold values from -0.125 to 0.125
- down_weight: bfloat16 [8192, 2048], P('tensor'), may hold values from -0.0625 to 0.0625
- cotangent: bfloat16 [8192, 2048], P('dp'), may hold values from -6 to 6
Outputs:
- block_output: bfloat16 [8192, 2048], P('dp')
- input_gradient: float32 [8192, 2048], P('dp')
- attention_gain_gradient: float32 [2048], P('dp')
- query_gradient: float32 [2048, 2048], P('dp', 'tensor')
- key_gradient: float32 [2048, 2048], P('dp', 'tensor')
- value_gradient: float32 [2048, 2048], P('dp', 'tensor')
- output_gradient: float32 [2048, 2048], P('tensor', 'dp')
- feedforward_gain_gradient: float32 [2048], P('dp')
- gate_gradient: float32 [2048, 8192], P('dp', 'tensor')
- up_gradient: float32 [2048, 8192], P('dp', 'tensor')
- down_gradient: float32 [8192, 2048], P('tensor', 'dp')
Inputs may be any that keep to these rules, and one draw needn't show every extreme that they name: `block_owner`: each sequence takes one to 4 consecutive blocks of a single index of dp; a block's entry is the index of its sequence's first block in the whole array. The first 4 blocks of every index of dp form one sequence. `token_mask`: in each sequence the real tokens come first and there is at least one unless the sequence is a single block of padding; the first sequence of every index of dp is all real (512 tokens). Blocks after the last real token of an index of dp are padding, each its own sequence.
All inputs are finite; a program needn't handle non-finite values.
Results may differ from a plain program's by a relative error of at most 0.014.
Values sent between devices are 32-bit elements; how exact they have to be, the bound alone decides.
No kernel may reach another device: no remote copies, remote signals or barrier semaphores. Data moves between devices by JAX's collectives and lax.ppermute only.
A program may use at most 384 MiB of HBM per device.

v0:
```python
import jax
import jax.numpy as jnp
from jax import lax
from jax.sharding import PartitionSpec as P

HD = 64
BLK = 128
GROUP = 512
WINDOW = 896
NORM_EPS = 1e-05
ROPE_BASE = 130000.0
MASKED = -1e30


def rms_forward(values, norm_gain):
    inverse = lax.rsqrt(jnp.mean(values * values, axis=-1, keepdims=True) + NORM_EPS)
    return (values * inverse * norm_gain, inverse)


def rms_backward(values, inverse, norm_gain, upstream):
    unit_rows = values * inverse
    gain_part = jnp.sum(upstream * unit_rows, axis=0)
    scaled = upstream * norm_gain
    back = inverse * (scaled - unit_rows * jnp.mean(scaled * unit_rows, axis=-1, keepdims=True))
    return (back, gain_part)


def rope_tables(positions, width):
    half_width = width // 2
    frequency = ROPE_BASE ** (-(jnp.arange(half_width, dtype=jnp.float32) * 2.0 / width))
    angles = positions.astype(jnp.float32)[:, None] * frequency[None, :]
    return (jnp.cos(angles)[:, None, :], jnp.sin(angles)[:, None, :])


def rotate(values, cosine, sine):
    half_width = values.shape[-1] // 2
    first_half = values[..., :half_width]
    second_half = values[..., half_width:]
    return jnp.concatenate(
        [first_half * cosine - second_half * sine, second_half * cosine + first_half * sine],
        axis=-1,
    )


def allowed_keys(query_owner, query_pos, key_owner, key_pos, key_valid):
    same = query_owner[:, None] == key_owner[None, :]
    causal = key_pos[None, :] <= query_pos[:, None]
    usable = (key_valid[None, :] > 0) | (key_pos[None, :] == 0)
    return same & causal & usable


def masked_scores(query_block, key_block, allowed, scale):
    scores = (
        jnp.einsum("qhd,khd->hqk", query_block, key_block, preferred_element_type=jnp.float32)
        * scale
    )
    return jnp.where(allowed[None], scores, MASKED)


def on_device(
    block_input,
    block_owner,
    token_mask,
    attention_gain,
    query_weight,
    key_weight,
    value_weight,
    output_weight,
    feedforward_gain,
    gate_weight,
    up_weight,
    down_weight,
    cotangent,
):
    row_count = block_input.shape[0]
    head_count = query_weight.shape[1] // HD
    scale = HD ** (-0.5)
    front = WINDOW - GROUP
    group_count = row_count // GROUP
    first_block = lax.axis_index("dp") * (row_count // BLK)
    owners = jnp.repeat(block_owner, BLK, total_repeat_length=row_count)
    row_index = jnp.arange(row_count, dtype=jnp.int32)
    positions = (row_index // BLK + first_block - owners) * BLK + row_index % BLK
    cosine, sine = rope_tables(positions, HD)
    key_owner = jnp.concatenate([jnp.full((front,), -1, jnp.int32), owners])
    key_pos = jnp.concatenate([jnp.zeros((front,), jnp.int32), positions])
    key_valid = jnp.concatenate([jnp.zeros((front,), jnp.int32), token_mask])
    group_masks = []
    for group in range(group_count):
        start = group * GROUP
        group_masks.append(
            allowed_keys(
                owners[start : start + GROUP],
                positions[start : start + GROUP],
                key_owner[start : start + WINDOW],
                key_pos[start : start + WINDOW],
                key_valid[start : start + WINDOW],
            )
        )
    inputs_f = block_input.astype(jnp.float32)
    normed_one, inverse_one = rms_forward(inputs_f, attention_gain)
    act_one = normed_one.astype(jnp.bfloat16)

    def project(weight):
        return jnp.dot(act_one, weight, preferred_element_type=jnp.float32).reshape(
            row_count, head_count, HD
        )

    queries = rotate(project(query_weight), cosine, sine).astype(jnp.bfloat16)
    keys_rot = rotate(project(key_weight), cosine, sine).astype(jnp.bfloat16)
    values_b = project(value_weight).astype(jnp.bfloat16)
    pad_block = jnp.zeros((front, head_count, HD), jnp.bfloat16)
    key_pad = jnp.concatenate([pad_block, keys_rot], axis=0)
    value_pad = jnp.concatenate([pad_block, values_b], axis=0)
    attn_list = []
    logsum_list = []
    for group in range(group_count):
        start = group * GROUP
        scores = masked_scores(
            queries[start : start + GROUP],
            key_pad[start : start + WINDOW],
            group_masks[group],
            scale,
        )
        peak = jnp.max(scores, axis=-1, keepdims=True)
        logsum = peak + jnp.log(jnp.sum(jnp.exp(scores - peak), axis=-1, keepdims=True))
        probs = jnp.exp(scores - logsum).astype(jnp.bfloat16)
        result = jnp.einsum(
            "hqk,khd->qhd",
            probs,
            value_pad[start : start + WINDOW],
            preferred_element_type=jnp.float32,
        )
        attn_list.append(result.astype(jnp.bfloat16))
        logsum_list.append(logsum)
    attn_heads = jnp.concatenate(attn_list, axis=0)
    attn_flat = attn_heads.reshape(row_count, head_count * HD)
    attn_part = jnp.dot(attn_flat, output_weight, preferred_element_type=jnp.float32)
    attn_total = lax.psum(attn_part, "tensor")
    hidden_sum = inputs_f + attn_total
    normed_two, inverse_two = rms_forward(hidden_sum, feedforward_gain)
    act_two = normed_two.astype(jnp.bfloat16)
    gate_pre = jnp.dot(act_two, gate_weight, preferred_element_type=jnp.float32)
    up_pre = jnp.dot(act_two, up_weight, preferred_element_type=jnp.float32)
    sigmoid_gate = jax.nn.sigmoid(gate_pre)
    inner = (gate_pre * sigmoid_gate * up_pre).astype(jnp.bfloat16)
    mlp_part = jnp.dot(inner, down_weight, preferred_element_type=jnp.float32)
    mlp_total = lax.psum(mlp_part, "tensor")
    block_output = (hidden_sum + mlp_total).astype(jnp.bfloat16)
    grad_rows = jnp.where(token_mask[:, None] > 0, cotangent, jnp.zeros_like(cotangent))
    down_grad = jnp.dot(inner.T, grad_rows, preferred_element_type=jnp.float32)
    inner_grad = jnp.dot(grad_rows, down_weight.T, preferred_element_type=jnp.float32)
    gate_back = (
        inner_grad * up_pre * sigmoid_gate * (1.0 + gate_pre * (1.0 - sigmoid_gate))
    ).astype(jnp.bfloat16)
    up_back = (inner_grad * gate_pre * sigmoid_gate).astype(jnp.bfloat16)
    gate_grad = jnp.dot(act_two.T, gate_back, preferred_element_type=jnp.float32)
    up_grad = jnp.dot(act_two.T, up_back, preferred_element_type=jnp.float32)
    act_two_part = jnp.dot(gate_back, gate_weight.T, preferred_element_type=jnp.float32) + jnp.dot(
        up_back, up_weight.T, preferred_element_type=jnp.float32
    )
    act_two_grad = lax.psum(act_two_part, "tensor")
    hidden_norm_back, second_gain_grad = rms_backward(
        hidden_sum, inverse_two, feedforward_gain, act_two_grad
    )
    hidden_grad = grad_rows.astype(jnp.float32) + hidden_norm_back
    mlp_summed = (
        lax.psum_scatter(gate_grad, "dp", scatter_dimension=0, tiled=True),
        lax.psum_scatter(up_grad, "dp", scatter_dimension=0, tiled=True),
        lax.psum_scatter(down_grad, "dp", scatter_dimension=1, tiled=True),
        lax.psum_scatter(second_gain_grad, "dp", scatter_dimension=0, tiled=True),
    )
    hidden_back = hidden_grad.astype(jnp.bfloat16)
    out_grad = jnp.dot(attn_flat.T, hidden_back, preferred_element_type=jnp.float32)
    attention_grad = (
        jnp.dot(hidden_back, output_weight.T, preferred_element_type=jnp.float32)
        .astype(jnp.bfloat16)
        .reshape(row_count, head_count, HD)
    )
    key_acc = jnp.zeros((front + row_count, head_count, HD), jnp.float32)
    value_acc = jnp.zeros((front + row_count, head_count, HD), jnp.float32)
    query_parts = []
    for group in range(group_count):
        start = group * GROUP
        query_block = queries[start : start + GROUP]
        key_block = key_pad[start : start + WINDOW]
        value_block = value_pad[start : start + WINDOW]
        grad_block = attention_grad[start : start + GROUP]
        scores = masked_scores(query_block, key_block, group_masks[group], scale)
        probs_f = jnp.exp(scores - logsum_list[group])
        probs_b = probs_f.astype(jnp.bfloat16)
        value_acc = value_acc.at[start : start + WINDOW].add(
            jnp.einsum("hqk,qhd->khd", probs_b, grad_block, preferred_element_type=jnp.float32)
        )
        prob_grad = jnp.einsum(
            "qhd,khd->hqk", grad_block, value_block, preferred_element_type=jnp.float32
        )
        delta = jnp.sum(
            grad_block.astype(jnp.float32) * attn_heads[start : start + GROUP].astype(jnp.float32),
            axis=-1,
        ).T[:, :, None]
        score_grad = (probs_f * (prob_grad - delta) * scale).astype(jnp.bfloat16)
        query_parts.append(
            jnp.einsum("hqk,khd->qhd", score_grad, key_block, preferred_element_type=jnp.float32)
        )
        key_acc = key_acc.at[start : start + WINDOW].add(
            jnp.einsum("hqk,qhd->khd", score_grad, query_block, preferred_element_type=jnp.float32)
        )
    query_back = (
        rotate(jnp.concatenate(query_parts, axis=0), cosine, -sine)
        .astype(jnp.bfloat16)
        .reshape(row_count, head_count * HD)
    )
    key_back = (
        rotate(key_acc[front:], cosine, -sine)
        .astype(jnp.bfloat16)
        .reshape(row_count, head_count * HD)
    )
    value_back = value_acc[front:].astype(jnp.bfloat16).reshape(row_count, head_count * HD)
    query_grad = jnp.dot(act_one.T, query_back, preferred_element_type=jnp.float32)
    key_grad = jnp.dot(act_one.T, key_back, preferred_element_type=jnp.float32)
    value_grad = jnp.dot(act_one.T, value_back, preferred_element_type=jnp.float32)
    act_one_part = (
        jnp.dot(query_back, query_weight.T, preferred_element_type=jnp.float32)
        + jnp.dot(key_back, key_weight.T, preferred_element_type=jnp.float32)
        + jnp.dot(value_back, value_weight.T, preferred_element_type=jnp.float32)
    )
    act_one_grad = lax.psum(act_one_part, "tensor")
    input_norm_back, first_gain_grad = rms_backward(
        inputs_f, inverse_one, attention_gain, act_one_grad
    )
    input_gradient = hidden_grad + input_norm_back
    first_summed = (
        lax.psum_scatter(first_gain_grad, "dp", scatter_dimension=0, tiled=True),
        lax.psum_scatter(query_grad, "dp", scatter_dimension=0, tiled=True),
        lax.psum_scatter(key_grad, "dp", scatter_dimension=0, tiled=True),
        lax.psum_scatter(value_grad, "dp", scatter_dimension=0, tiled=True),
        lax.psum_scatter(out_grad, "dp", scatter_dimension=1, tiled=True),
    )
    gate_sum, up_sum, down_sum, second_gain_sum = mlp_summed
    first_gain_sum, query_sum, key_sum, value_sum, out_sum = first_summed
    return (
        block_output,
        input_gradient,
        first_gain_sum,
        query_sum,
        key_sum,
        value_sum,
        out_sum,
        second_gain_sum,
        gate_sum,
        up_sum,
        down_sum,
    )


def solution(mesh):
    return jax.shard_map(
        on_device,
        mesh=mesh,
        in_specs=(
            P("dp", None),
            P("dp"),
            P("dp"),
            P(),
            P(None, "tensor"),
            P(None, "tensor"),
            P(None, "tensor"),
            P("tensor", None),
            P(),
            P(None, "tensor"),
            P(None, "tensor"),
            P("tensor", None),
            P("dp", None),
        ),
        out_specs=(
            P("dp", None),
            P("dp", None),
            P("dp"),
            P("dp", "tensor"),
            P("dp", "tensor"),
            P("dp", "tensor"),
            P("tensor", "dp"),
            P("dp"),
            P("dp", "tensor"),
            P("dp", "tensor"),
            P("tensor", "dp"),
        ),
        check_vma=False,
    )
```

profile of v0, /device:TPU:0, one launch (start us, length us, event | category | flops | bytes accessed | tf_op | source)
XLA Modules:
  0.0 1614.1 jit_solution(13321575594222905438)
XLA Ops:
  7.3 1.6 fusion.80
  8.9 4.5 compare_select_fusion.1
  13.4 0.7 fusion.75
  14.1 3.1 fusion.14
  17.2 5.5 fusion.72
  22.8 2.6 fusion.70
  25.4 1.2 fusion.31
  26.6 0.7 add_convert_fusion.3
  28.0 2.8 fusion.6
  30.8 4.0 exponential_reduce_fusion.1
  34.8 2.6 convolution_convert_fusion
  38.0 6.8 fusion.7
  44.8 7.3 exponential_reduce_fusion
  52.3 4.1 fusion.24
  56.4 7.5 fusion.25
  64.1 0.7 copy-done.25
  64.7 1.0 copy-done.31
  65.7 5.8 fusion.81
  71.6 174.8 %all-reduce.15.cloned.1.call-done = f32[1024,2048]{1,0:T(8,128)} async-done(((f32[1024,2048]{1,0:T(8,128)}), f32[1024,2048]{1,0:T(8,128)}) %all-reduce.15.cloned.1.call-update) | async-done | bytes 8388624 | tf_op jit(solution)/shard_map/psum | solution.py:139
  246.5 5.7 multiply_reduce_fusion.2
  252.2 0.7 multiply_convert_fusion.5
  253.0 16.5 %fusion.82 = f32[1024,2048]{1,0:T(8,128)} fusion(bf16[1024,2048]{1,0:T(8,128)(2,1)S(1)} %multiply_convert_fusion.5, bf16[2048,2048]{1,0:T(8,128)(2,1)} %param.32), kind=kOutput, calls=%fused_computation.154 | convolution fusion | flops 8589934592 | bytes 20971520 | tf_op jit(solution)/shard_map/dot_general | solution.py:143
  269.5 13.3 fusion.83
  282.9 21.9 %multiply_convert_fusion.2 = (bf16[1024,2048]{1,0:T(8,128)(2,1)}, bf16[1024,2048]{1,0:T(8,128)(2,1)}, bf16[1024,2048]{1,0:T(8,128)(2,1)}) fusion(f32[1024,2048]{1,0:T(8,128)} %fusion.82, f32[1024,2048]{1,0:T(8,128)} %fusion.83, bf16[2048,2048]{1,0:T(8,128)(2,1)} %param.34, bf16[1024,2048]{1,0:T(8,128)(2,1)} %param.35, ...), kind=kOutput, calls=%fused_computation.30 | convolution fusion | flops 8625586176 | bytes 41944064 | tf_op jit(solution)/shard_map/dot_general | solution.py:152
  304.8 13.1 fusion.85
  317.9 13.6 convolution_add_fusion
  331.6 14.7 fusion.84
  346.3 158.2 %all-reduce.17.cloned.1.call-done = f32[1024,2048]{1,0:T(8,128)} async-done(((f32[1024,2048]{1,0:T(8,128)}), f32[1024,2048]{1,0:T(8,128)}) %all-reduce.17.cloned.1.call-update) | async-done | bytes 8388624 | tf_op jit(solution)/shard_map/psum | solution.py:162
  504.4 7.6 multiply_reduce_fusion
  512.1 9.5 multiply_add_fusion
  521.7 6.6 fusion.21
  528.8 4.0 convolution_bitcast_fusion
  532.9 7.6 multiply_convert_fusion.1
  540.5 5.6 convolution_bitcast_fusion.3
  546.1 1.4 convolution_bitcast_fusion.1
  547.8 7.4 fusion.19
  555.4 9.1 multiply_convert_fusion
  564.6 2.3 convolution_bitcast_fusion.2
  567.2 1.5 fusion.20
  569.5 1.0 copy-done.35
  570.4 2.4 fusion.87
  572.9 1.0 copy-done.33
  573.9 2.4 fusion.86
  576.3 5.8 add_add_fusion
  582.9 7.2 fusion.64
  590.1 7.8 fusion.15
  598.0 7.0 fusion.66
  605.1 7.3 fusion.68
  612.6 15.6 fusion.88
  628.3 15.5 fusion.89
  644.2 15.6 fusion.62
  661.7 228.7 %all-reduce.19.cloned.1.call-done = (f32[1024,2048]{1,0:T(8,128)}, f32[1024,2048]{1,0:T(8,128)}) async-done(((f32[1024,2048]{1,0:T(8,128)}, f32[1024,2048]{1,0:T(8,128)}), (f32[1024,2048]{1,0:T(8,128)}, f32[1024,2048]{1,0:T(8,128)})) %all-reduce.19.cloned.1.call-update) | async-done | bytes 16777232 | tf_op jit(solution)/shard_map/psum | solution.py:148
  890.4 5.9 fusion.13
  896.2 29.6 %all-reduce.9 = (f32[2048]{0:T(1024)S(1)}, f32[2048]{0:T(1024)S(1)}) all-reduce(f32[2048]{0:T(1024)S(1)} %get-tuple-element.73, f32[2048]{0:T(1024)S(1)} %copy-done.47), channel_id=2, replica_groups=mesh['dp'=8,'tensor'=4] {'dp'}, use_global_device_ids=true, to_apply=%region_15.16.clone | all-reduce | flops 4096 | bytes 32768
  925.8 0.6 dynamic-slice.41
  926.5 0.6 dynamic-slice.43
  927.1 9.6 add_convert_fusion
  936.7 9.8 fusion.12
  946.6 49.2 %reduce-scatter.14.cloned.1.call-done = f32[512,256]{1,0:T(8,128)} async-done(((f32[512,2048]{1,0:T(8,128)}), f32[512,256]{1,0:T(8,128)}) %reduce-scatter.14.cloned.1.call-update) | async-done | bytes 524304 | tf_op jit(solution)/shard_map/reduce_scatter | solution.py:238
  995.8 51.1 %reduce-scatter.10.cloned.1.call-done = f32[256,512]{1,0:T(8,128)} async-done(((f32[2048,512]{1,0:T(8,128)}), f32[256,512]{1,0:T(8,128)}) %reduce-scatter.10.cloned.1.call-update) | async-done | bytes 524304 | tf_op jit(solution)/shard_map/reduce_scatter | solution.py:236
  1046.9 51.3 %reduce-scatter.8.cloned.1.call-done = f32[256,512]{1,0:T(8,128)} async-done(((f32[2048,512]{1,0:T(8,128)}), f32[256,512]{1,0:T(8,128)}) %reduce-scatter.8.cloned.1.call-update) | async-done | bytes 524304 | tf_op jit(solution)/shard_map/reduce_scatter | solution.py:235
  1098.2 169.6 %reduce-scatter.16.cloned.1.call-done = f32[256,2048]{1,0:T(8,128)} async-done(((f32[2048,2048]{1,0:T(8,128)}), f32[256,2048]{1,0:T(8,128)}) %reduce-scatter.16.cloned.1.call-update) | async-done | bytes 2097168 | tf_op jit(solution)/shard_map/reduce_scatter | solution.py:168
  1267.8 169.6 %reduce-scatter.18.cloned.1.call-done = f32[256,2048]{1,0:T(8,128)} async-done(((f32[2048,2048]{1,0:T(8,128)}), f32[256,2048]{1,0:T(8,128)}) %reduce-scatter.18.cloned.1.call-update) | async-done | bytes 2097168 | tf_op jit(solution)/shard_map/reduce_scatter | solution.py:169
  1437.4 169.4 %reduce-scatter.20.cloned.1.call-done = f32[2048,256]{1,0:T(8,128)} async-done(((f32[2048,2048]{1,0:T(8,128)}), f32[2048,256]{1,0:T(8,128)}) %reduce-scatter.20.cloned.1.call-update) | async-done | bytes 2097168 | tf_op jit(solution)/shard_map/reduce_scatter | solution.py:170
  (172 shorter events, 6.3 us)
Async XLA Ops:
  7.2 58.5 %copy-start = (bf16[512,2048]{1,0:T(8,128)(2,1)S(1)}, bf16[512,2048]{1,0:T(8,128)(2,1)}, u32[]{:S(2)}) copy-start(bf16[512,2048]{1,0:T(8,128)(2,1)} %param.30) | copy-start | bytes 6291460
  7.2 239.3 %all-reduce.15.cloned.1.call-start = ((), (), s32[]{:S(2)}) async-start(), calls=%async_computation.7 | async-start | bytes 16777216 | tf_op jit(solution)/shard_map/psum | solution.py:139
  17.2 17.6 %copy-start.44 = (f32[1024]{0:T(1024)}, f32[1024]{0:T(1024)S(1)}, u32[]{:S(2)}) copy-start(f32[1024]{0:T(1024)S(1)} %add_rsqrt_fusion.1) | copy-start | bytes 12292
  17.2 5.5 copy-start.3
  17.2 5.5 copy-start.48
  17.2 5.5 copy-start.54
  22.8 2.6 copy-start.46
  27.3 10.7 copy-start.9
  27.4 10.6 copy-start.11
  27.4 10.6 copy-start.13
  27.4 10.6 copy-start.15
  27.5 3.3 copy-start.7
  28.0 24.2 %copy-start.19 = (pred[512,896]{1,0:T(8,128)(4,1)}, pred[512,896]{1,0:T(8,128)(4,1)S(1)}, u32[]{:S(2)}) copy-start(pred[512,896]{1,0:T(8,128)(4,1)S(1)} %and_and_fusion.1) | copy-start | bytes 1376260
  30.8 21.4 %copy-start.5 = (f32[8,512,896]{2,1,0:T(8,128)}, f32[8,512,896]{2,1,0:T(8,128)S(1)}, u32[]{:S(2)}) copy-start(f32[8,512,896]{2,1,0:T(8,128)S(1)} %get-tuple-element.127) | copy-start | bytes 44040196
  30.8 4.0 copy-start.21
  34.8 17.4 %copy-start.52 = (f32[8,512]{1,0:T(8,128)}, f32[8,512]{1,0:T(8,128)S(1)}, u32[]{:S(2)}) copy-start(f32[8,512]{1,0:T(8,128)S(1)} %log_add_fusion.1) | copy-start | bytes 49156
  37.5 14.8 copy-start.39
  38.0 18.4 %copy-start.27 = (pred[512,896]{1,0:T(8,128)(4,1)}, pred[512,896]{1,0:T(8,128)(4,1)S(1)}, u32[]{:S(2)}) copy-start(pred[512,896]{1,0:T(8,128)(4,1)S(1)} %and_and_fusion) | copy-start | bytes 1376260
  52.1 4.3 copy-start.50
  52.2 4.2 copy-start.37
  56.4 7.5 copy-start.23
  71.5 432.9 %all-reduce.17.cloned.1.call-start = ((), (), s32[]{:S(2)}) async-start(), calls=%async_computation.8 | async-start | bytes 16777216 | tf_op jit(solution)/shard_map/psum | solution.py:162
  71.6 180.6 %copy-start.43 = (f32[2048]{0:T(1024)S(1)}, f32[2048]{0:T(1024)}, u32[]{:S(2)}) copy-start(f32[2048]{0:T(1024)} %param.31) | copy-start | bytes 24580
  252.2 17.4 %copy-start.2 = (f32[1024,2048]{1,0:T(8,128)}, f32[1024,2048]{1,0:T(8,128)S(1)}, u32[]{:S(2)}) copy-start(f32[1024,2048]{1,0:T(8,128)S(1)} %get-tuple-element.82) | copy-start | bytes 25165828
  253.0 16.6 %copy-start.17 = (bf16[1024,2048]{1,0:T(8,128)(2,1)}, bf16[1024,2048]{1,0:T(8,128)(2,1)S(1)}, u32[]{:S(2)}) copy-start(bf16[1024,2048]{1,0:T(8,128)(2,1)S(1)} %multiply_convert_fusion.5) | copy-start | bytes 12582916
  304.8 13.2 copy-start.58
  331.5 558.8 %all-reduce.19.cloned.1.call-start = ((), (), s32[]{:S(2)}) async-start(), calls=%async_computation.16 | async-start | bytes 33554432 | tf_op jit(solution)/shard_map/psum | solution.py:148
  504.4 7.6 copy-start.18
  512.1 16.7 %slice-start = ((s8[14680064]{0:T(1024)(128)(4,1)}), s8[4194304]{0:T(1024)(128)(4,1)S(1)}, s32[]{:S(2)}) async-start(s8[14680064]{0:T(1024)(128)(4,1)} %bitcast.98), calls=%async_computation.17 | async-start | bytes 8388608
  512.1 16.7 %slice-start.1 = ((s8[14680064]{0:T(1024)(128)(4,1)}), s8[4194304]{0:T(1024)(128)(4,1)S(1)}, s32[]{:S(2)}) async-start(s8[14680064]{0:T(1024)(128)(4,1)} %bitcast.98), calls=%async_computation.18 | async-start | bytes 8388608
  512.1 16.7 %slice-start.2 = ((s8[14680064]{0:T(1024)(128)(4,1)}), s8[4194304]{0:T(1024)(128)(4,1)S(1)}, s32[]{:S(2)}) async-start(s8[14680064]{0:T(1024)(128)(4,1)} %bitcast.98), calls=%async_computation.19 | async-start | bytes 8388608
  521.6 6.7 copy-start.24
  521.6 6.7 copy-start.26
  521.6 7.1 slice-start.3
  521.6 7.1 copy-start.20
  521.6 7.1 copy-start.53
  528.4 19.3 %copy-start.42 = (bf16[512,512]{0,1:T(8,128)(2,1)}, bf16[512,512]{0,1:T(8,128)(2,1)S(1)}, u32[]{:S(2)}) copy-start(bf16[512,512]{0,1:T(8,128)(2,1)S(1)} %get-tuple-element.98) | copy-start | bytes 1572868
  528.8 4.0 copy-start.40
  532.9 7.6 copy-start.8
  540.4 5.6 copy-start.6
  540.5 5.6 copy-start.10
  540.5 5.6 copy-start.12
  546.1 1.7 copy-start.28
  546.1 1.7 copy-start.51
  547.7 7.6 copy-start.38
  555.4 9.2 copy-start.14
  555.4 9.2 copy-start.16
  567.2 1.5 copy-start.30
  568.7 1.7 copy-start.55
  569.4 4.5 copy-start.56
  572.8 3.5 copy-start.22
  582.2 7.9 copy-start.32
  582.2 364.4 %reduce-scatter.12.cloned.1.call-start = ((), (), s32[]{:S(2)}) async-start(), calls=%async_computation.11 | async-start | bytes 4718592 | tf_op jit(solution)/shard_map/reduce_scatter | solution.py:237
  590.1 7.9 copy-start.36
  590.1 405.7 %reduce-scatter.14.cloned.1.call-start = ((), (), s32[]{:S(2)}) async-start(), calls=%async_computation.12 | async-start | bytes 4718592 | tf_op jit(solution)/shard_map/reduce_scatter | solution.py:238
  597.9 7.2 copy-start.34
  597.9 449.0 %reduce-scatter.10.cloned.1.call-start = ((), (), s32[]{:S(2)}) async-start(), calls=%async_computation.10 | async-start | bytes 4718592 | tf_op jit(solution)/shard_map/reduce_scatter | solution.py:236
  605.0 493.2 %reduce-scatter.8.cloned.1.call-start = ((), (), s32[]{:S(2)}) async-start(), calls=%async_computation.9 | async-start | bytes 4718592 | tf_op jit(solution)/shard_map/reduce_scatter | solution.py:235
  612.4 655.4 %reduce-scatter.16.cloned.1.call-start = ((), (), s32[]{:S(2)}) async-start(), calls=%async_computation.13 | async-start | bytes 18874368 | tf_op jit(solution)/shard_map/reduce_scatter | solution.py:168
  628.3 809.1 %reduce-scatter.18.cloned.1.call-start = ((), (), s32[]{:S(2)}) async-start(), calls=%async_computation.14 | async-start | bytes 18874368 | tf_op jit(solution)/shard_map/reduce_scatter | solution.py:169
  643.9 963.0 %reduce-scatter.20.cloned.1.call-start = ((), (), s32[]{:S(2)}) async-start(), calls=%async_computation.15 | async-start | bytes 18874368 | tf_op jit(solution)/shard_map/reduce_scatter | solution.py:170
  659.8 236.4 %copy-start.47 = (f32[2048]{0:T(1024)S(1)}, f32[2048]{0:T(1024)}, u32[]{:S(2)}) copy-start(f32[2048]{0:T(1024)} %get-tuple-element.71) | copy-start | bytes 24580
  927.1 9.6 copy-start.4
  927.1 679.7 %copy-start.1 = (bf16[512,2048]{1,0:T(8,128)(2,1)S(1)}, bf16[512,2048]{1,0:T(8,128)(2,1)}, u32[]{:S(2)}) copy-start(bf16[512,2048]{1,0:T(8,128)(2,1)} %param.30) | copy-start | bytes 6291460
  (9 other events, 8.7 us)
Sparse Core Ops, SparseCore 0:
  71.7 174.7 all-reduce.14
  331.7 172.7 all-reduce.16
  582.3 308.0 all-reduce.18
  893.1 51.4 reduce-scatter.11
  947.3 48.4 reduce-scatter.13
  998.5 48.3 reduce-scatter.9
  1049.8 48.3 reduce-scatter.7
  1101.2 166.6 reduce-scatter.15
  1270.8 166.6 reduce-scatter.17
  1440.2 166.6 reduce-scatter.19
where the time goes:
time: 1620 us; the launch traced here: 1610 us
  waiting for transfers between devices  1220 us (75%)
  matrix products  263 us (16%)
  other arithmetic  72.8 us (4%)
  blocking collectives  29.6 us (2%)
  between operations  16.4 us (1%)
    psum x1, waiting for transfers between devices, on_device(): mlp_total = lax.psum(mlp_part, 'tensor')  229 us
    psum x1, waiting for transfers between devices, on_device(): attn_total = lax.psum(attn_part, 'tensor')  175 us
    reduce_scatter x1, waiting for transfers between devices, on_device(): lax.psum_scatter(up_grad, 'dp', scatter_dimension=0, tiled=True)  170 us
    reduce_scatter x1, waiting for transfers between devices, on_device(): lax.psum_scatter(gate_grad, 'dp', scatter_dimension=0, tiled=True)  170 us
    reduce_scatter x1, waiting for transfers between devices, on_device(): lax.psum_scatter(down_grad, 'dp', scatter_dimension=1, tiled=True)  169 us
    psum x1, waiting for transfers between devices, on_device(): act_two_grad = lax.psum(act_two_part, 'tensor')  158 us
    reduce_scatter x1, waiting for transfers between devices, on_device(): lax.psum_scatter(query_grad, 'dp', scatter_dimension=0, tiled=True)  51.3 us
    reduce_scatter x1, waiting for transfers between devices, on_device(): lax.psum_scatter(key_grad, 'dp', scatter_dimension=0, tiled=True)  51.1 us
  transfers between devices with their start and end apart: 10, of which 9 were waited for; matrix products, arithmetic and copies ran while one was open for 7% of the time, Pallas kernels for 0%

commit v1 on v0

--- a/solution.py
+++ b/solution.py
@@ -136,7 +136,7 @@
     attn_heads = jnp.concatenate(attn_list, axis=0)
     attn_flat = attn_heads.reshape(row_count, head_count * HD)
     attn_part = jnp.dot(attn_flat, output_weight, preferred_element_type=jnp.float32)
-    attn_total = lax.psum(attn_part, "tensor")
+    attn_total = jnp.sum(lax.all_gather(attn_part, "tensor"), axis=0)
     hidden_sum = inputs_f + attn_total
     normed_two, inverse_two = rms_forward(hidden_sum, feedforward_gain)
     act_two = normed_two.astype(jnp.bfloat16)

time: 1620 us -> 1760 us (1.086)
  waiting for transfers between devices: 1220 us -> 1350 us
    all_gather x0 -> x1, waiting for transfers between devices: none -> 300 us  [on_device(): attn_total = jnp.sum(lax.all_gather(attn_part, 'tensor'), axis=0)]
    psum x1 -> x0, waiting for transfers between devices: 175 us -> none  [on_device(): attn_total = lax.psum(attn_part, 'tensor')]
where the time goes in v1:
time: 1760 us; the launch traced here: 1750 us
  waiting for transfers between devices  1350 us (77%)
  matrix products  263 us (15%)
  other arithmetic  89.2 us (5%)
  blocking collectives  29.6 us (2%)
    all_gather x1, waiting for transfers between devices, on_device(): attn_total = jnp.sum(lax.all_gather(attn_part, 'tensor'), axis=0)  300 us
    psum x1, waiting for transfers between devices, on_device(): mlp_total = lax.psum(mlp_part, 'tensor')  229 us
    reduce_scatter x1, waiting for transfers between devices, on_device(): lax.psum_scatter(up_grad, 'dp', scatter_dimension=0, tiled=True)  170 us
    reduce_scatter x1, waiting for transfers between devices, on_device(): lax.psum_scatter(gate_grad, 'dp', scatter_dimension=0, tiled=True)  170 us
    reduce_scatter x1, waiting for transfers between devices, on_device(): lax.psum_scatter(down_grad, 'dp', scatter_dimension=1, tiled=True)  169 us
    psum x1, waiting for transfers between devices, on_device(): act_two_grad = lax.psum(act_two_part, 'tensor')  157 us
    reduce_scatter x1, waiting for transfers between devices, on_device(): lax.psum_scatter(query_grad, 'dp', scatter_dimension=0, tiled=True)  51.3 us
    reduce_scatter x1, waiting for transfers between devices, on_device(): lax.psum_scatter(key_grad, 'dp', scatter_dimension=0, tiled=True)  51.1 us
  transfers between devices with their start and end apart: 10, of which 9 were waited for; matrix products, arithmetic and copies ran while one was open for 7% of the time, Pallas kernels for 0%

profile of v1, /device:TPU:0, one launch (start us, length us, event | category | flops | bytes accessed | tf_op | source)
XLA Modules:
  0.0 1754.2 jit_solution(14434763133465057332)
XLA Ops:
  7.3 1.6 fusion.80
  8.9 4.5 compare_select_fusion.1
  13.4 0.7 fusion.75
  14.1 3.1 fusion.14
  17.2 5.5 fusion.72
  22.8 2.6 fusion.70
  25.4 1.2 fusion.31
  26.6 0.7 add_convert_fusion.3
  28.0 2.8 fusion.6
  30.8 4.3 exponential_reduce_fusion.1
  35.1 2.6 convolution_convert_fusion
  38.3 6.8 fusion.7
  45.1 7.3 exponential_reduce_fusion
  52.5 4.1 fusion.24
  56.7 7.4 fusion.25
  64.3 0.7 copy-done.25
  65.0 1.0 copy-done.31
  66.0 5.8 fusion.81
  71.8 299.9 %all-gather.3.cloned.1.call-done = f32[4096,2048]{1,0:T(8,128)} async-done(((f32[1024,2048]{1,0:T(8,128)}), f32[4096,2048]{1,0:T(8,128)}) %all-gather.3.cloned.1.call-update) | async-done | bytes 33554448 | tf_op jit(solution)/shard_map/all_gather | solution.py:139
  371.7 16.1 reduce_sum.102
  387.9 5.7 multiply_reduce_fusion.2
  393.7 0.7 multiply_convert_fusion.5
  394.4 16.5 fusion.82
  410.9 13.4 fusion.83
  424.3 22.1 %multiply_convert_fusion.2 = (bf16[1024,2048]{1,0:T(8,128)(2,1)}, bf16[1024,2048]{1,0:T(8,128)(2,1)}, bf16[1024,2048]{1,0:T(8,128)(2,1)}) fusion(f32[1024,2048]{1,0:T(8,128)} %fusion.82, f32[1024,2048]{1,0:T(8,128)} %fusion.83, bf16[2048,2048]{1,0:T(8,128)(2,1)} %param.34, bf16[1024,2048]{1,0:T(8,128)(2,1)} %param.35, ...), kind=kOutput, calls=%fused_computation.30 | convolution fusion | flops 8625586176 | bytes 41944064 | tf_op jit(solution)/shard_map/dot_general | solution.py:152
  446.3 12.7 fusion.85
  459.1 13.7 convolution_add_fusion
  472.8 14.9 fusion.84
  487.7 157.2 %all-reduce.14.cloned.1.call-done = f32[1024,2048]{1,0:T(8,128)} async-done(((f32[1024,2048]{1,0:T(8,128)}), f32[1024,2048]{1,0:T(8,128)}) %all-reduce.14.cloned.1.call-update) | async-done | bytes 8388624 | tf_op jit(solution)/shard_map/psum | solution.py:162
  645.0 7.6 multiply_reduce_fusion
  652.6 9.5 multiply_add_fusion
  662.2 6.6 fusion.21
  669.3 4.0 convolution_bitcast_fusion
  673.4 7.5 multiply_convert_fusion.1
  680.9 5.6 convolution_bitcast_fusion.3
  686.6 1.4 convolution_bitcast_fusion.1
  688.2 7.4 fusion.19
  695.9 9.0 multiply_convert_fusion
  704.8 2.3 convolution_bitcast_fusion.2
  707.5 1.5 fusion.20
  709.7 1.0 copy-done.35
  710.7 2.4 fusion.87
  713.2 1.0 copy-done.33
  714.2 2.4 fusion.86
  716.6 5.9 add_add_fusion
  723.2 7.2 fusion.64
  730.4 7.8 fusion.15
  738.3 7.0 fusion.66
  745.4 7.3 fusion.68
  752.9 15.6 fusion.88
  768.6 15.5 fusion.89
  784.4 15.6 fusion.62
  801.9 228.8 %all-reduce.16.cloned.1.call-done = (f32[1024,2048]{1,0:T(8,128)}, f32[1024,2048]{1,0:T(8,128)}) async-done(((f32[1024,2048]{1,0:T(8,128)}, f32[1024,2048]{1,0:T(8,128)}), (f32[1024,2048]{1,0:T(8,128)}, f32[1024,2048]{1,0:T(8,128)})) %all-reduce.16.cloned.1.call-update) | async-done | bytes 16777232 | tf_op jit(solution)/shard_map/psum | solution.py:148
  1030.7 5.9 fusion.13
  1036.5 29.6 %all-reduce.9 = (f32[2048]{0:T(1024)S(1)}, f32[2048]{0:T(1024)S(1)}) all-reduce(f32[2048]{0:T(1024)S(1)} %get-tuple-element.73, f32[2048]{0:T(1024)S(1)} %copy-done.47), channel_id=3, replica_groups=mesh['dp'=8,'tensor'=4] {'dp'}, use_global_device_ids=true, to_apply=%region_15.16.clone | all-reduce | flops 4096 | bytes 32768
  1066.1 0.6 dynamic-slice.41
  1067.4 9.6 add_convert_fusion
  1077.1 9.8 fusion.12
  1086.9 49.2 %reduce-scatter.14.cloned.1.call-done = f32[512,256]{1,0:T(8,128)} async-done(((f32[512,2048]{1,0:T(8,128)}), f32[512,256]{1,0:T(8,128)}) %reduce-scatter.14.cloned.1.call-update) | async-done | bytes 524304 | tf_op jit(solution)/shard_map/reduce_scatter | solution.py:238
  1136.1 51.1 %reduce-scatter.10.cloned.1.call-done = f32[256,512]{1,0:T(8,128)} async-done(((f32[2048,512]{1,0:T(8,128)}), f32[256,512]{1,0:T(8,128)}) %reduce-scatter.10.cloned.1.call-update) | async-done | bytes 524304 | tf_op jit(solution)/shard_map/reduce_scatter | solution.py:236
  1187.3 51.3 %reduce-scatter.8.cloned.1.call-done = f32[256,512]{1,0:T(8,128)} async-done(((f32[2048,512]{1,0:T(8,128)}), f32[256,512]{1,0:T(8,128)}) %reduce-scatter.8.cloned.1.call-update) | async-done | bytes 524304 | tf_op jit(solution)/shard_map/reduce_scatter | solution.py:235
  1238.5 169.6 %reduce-scatter.16.cloned.1.call-done = f32[256,2048]{1,0:T(8,128)} async-done(((f32[2048,2048]{1,0:T(8,128)}), f32[256,2048]{1,0:T(8,128)}) %reduce-scatter.16.cloned.1.call-update) | async-done | bytes 2097168 | tf_op jit(solution)/shard_map/reduce_scatter | solution.py:168
  1408.1 169.6 %reduce-scatter.18.cloned.1.call-done = f32[256,2048]{1,0:T(8,128)} async-done(((f32[2048,2048]{1,0:T(8,128)}), f32[256,2048]{1,0:T(8,128)}) %reduce-scatter.18.cloned.1.call-update) | async-done | bytes 2097168 | tf_op jit(solution)/shard_map/reduce_scatter | solution.py:169
  1577.7 169.4 %reduce-scatter.20.cloned.1.call-done = f32[2048,256]{1,0:T(8,128)} async-done(((f32[2048,2048]{1,0:T(8,128)}), f32[2048,256]{1,0:T(8,128)}) %reduce-scatter.20.cloned.1.call-update) | async-done | bytes 2097168 | tf_op jit(solution)/shard_map/reduce_scatter | solution.py:170
  (173 shorter events, 6.9 us)
Async XLA Ops:
  7.2 58.8 %copy-start = (bf16[512,2048]{1,0:T(8,128)(2,1)S(1)}, bf16[512,2048]{1,0:T(8,128)(2,1)}, u32[]{:S(2)}) copy-start(bf16[512,2048]{1,0:T(8,128)(2,1)} %param.30) | copy-start | bytes 6291460
  7.2 364.6 %all-gather.3.cloned.1.call-start = ((), (), s32[]{:S(2)}) async-start(), calls=%async_computation.15 | async-start | bytes 41943040 | tf_op jit(solution)/shard_map/all_gather | solution.py:139
  17.2 17.9 %copy-start.44 = (f32[1024]{0:T(1024)}, f32[1024]{0:T(1024)S(1)}, u32[]{:S(2)}) copy-start(f32[1024]{0:T(1024)S(1)} %add_rsqrt_fusion.1) | copy-start | bytes 12292
  17.2 5.5 copy-start.3
  17.2 5.5 copy-start.48
  17.2 5.5 copy-start.54
  22.8 2.6 copy-start.46
  27.3 10.9 copy-start.9
  27.3 10.9 copy-start.11
  27.4 10.9 copy-start.13
  27.4 10.9 copy-start.15
  27.5 3.3 copy-start.7
  28.0 24.5 %copy-start.19 = (pred[512,896]{1,0:T(8,128)(4,1)}, pred[512,896]{1,0:T(8,128)(4,1)S(1)}, u32[]{:S(2)}) copy-start(pred[512,896]{1,0:T(8,128)(4,1)S(1)} %and_and_fusion.1) | copy-start | bytes 1376260
  30.8 21.7 %copy-start.5 = (f32[8,512,896]{2,1,0:T(8,128)}, f32[8,512,896]{2,1,0:T(8,128)S(1)}, u32[]{:S(2)}) copy-start(f32[8,512,896]{2,1,0:T(8,128)S(1)} %get-tuple-element.127) | copy-start | bytes 44040196
  30.8 4.3 copy-start.21
  35.1 17.4 copy-start.52
  37.8 14.8 copy-start.39
  38.3 18.4 %copy-start.27 = (pred[512,896]{1,0:T(8,128)(4,1)}, pred[512,896]{1,0:T(8,128)(4,1)S(1)}, u32[]{:S(2)}) copy-start(pred[512,896]{1,0:T(8,128)(4,1)S(1)} %and_and_fusion) | copy-start | bytes 1376260
  52.4 4.3 copy-start.50
  52.5 4.2 copy-start.37
  56.7 7.5 copy-start.23
  71.8 573.2 %all-reduce.14.cloned.1.call-start = ((), (), s32[]{:S(2)}) async-start(), calls=%async_computation.7 | async-start | bytes 16777216 | tf_op jit(solution)/shard_map/psum | solution.py:162
  387.9 5.8 copy-start.43
  393.6 17.3 copy-start.2
  394.4 16.5 copy-start.17
  446.3 12.7 copy-start.58
  472.8 557.9 %all-reduce.16.cloned.1.call-start = ((), (), s32[]{:S(2)}) async-start(), calls=%async_computation.16 | async-start | bytes 33554432 | tf_op jit(solution)/shard_map/psum | solution.py:148
  644.9 7.6 copy-start.18
  652.6 16.7 slice-start
  652.6 16.7 slice-start.1
  652.6 16.7 slice-start.2
  662.1 6.7 copy-start.24
  662.1 6.7 copy-start.26
  662.1 7.1 slice-start.3
  662.1 7.1 copy-start.20
  662.1 7.1 copy-start.53
  668.9 19.3 %copy-start.42 = (bf16[512,512]{0,1:T(8,128)(2,1)}, bf16[512,512]{0,1:T(8,128)(2,1)S(1)}, u32[]{:S(2)}) copy-start(bf16[512,512]{0,1:T(8,128)(2,1)S(1)} %get-tuple-element.98) | copy-start | bytes 1572868
  669.3 4.0 copy-start.40
  673.4 7.6 copy-start.8
  680.9 5.6 copy-start.6
  680.9 5.6 copy-start.10
  680.9 5.6 copy-start.12
  686.5 1.7 copy-start.28
  686.5 1.7 copy-start.51
  688.2 7.6 copy-start.38
  695.8 9.0 copy-start.14
  695.9 9.0 copy-start.16
  707.4 1.5 copy-start.30
  709.0 1.7 copy-start.55
  709.6 4.5 copy-start.56
  713.1 3.5 copy-start.22
  722.5 7.9 copy-start.32
  722.5 364.4 %reduce-scatter.12.cloned.1.call-start = ((), (), s32[]{:S(2)}) async-start(), calls=%async_computation.10 | async-start | bytes 4718592 | tf_op jit(solution)/shard_map/reduce_scatter | solution.py:237
  730.4 7.9 copy-start.36
  730.4 405.7 %reduce-scatter.14.cloned.1.call-start = ((), (), s32[]{:S(2)}) async-start(), calls=%async_computation.11 | async-start | bytes 4718592 | tf_op jit(solution)/shard_map/reduce_scatter | solution.py:238
  738.2 7.2 copy-start.34
  738.3 449.0 %reduce-scatter.10.cloned.1.call-start = ((), (), s32[]{:S(2)}) async-start(), calls=%async_computation.9 | async-start | bytes 4718592 | tf_op jit(solution)/shard_map/reduce_scatter | solution.py:236
  745.4 493.2 %reduce-scatter.8.cloned.1.call-start = ((), (), s32[]{:S(2)}) async-start(), calls=%async_computation.8 | async-start | bytes 4718592 | tf_op jit(solution)/shard_map/reduce_scatter | solution.py:235
  752.7 655.4 %reduce-scatter.16.cloned.1.call-start = ((), (), s32[]{:S(2)}) async-start(), calls=%async_computation.12 | async-start | bytes 18874368 | tf_op jit(solution)/shard_map/reduce_scatter | solution.py:168
  768.5 809.2 %reduce-scatter.18.cloned.1.call-start = ((), (), s32[]{:S(2)}) async-start(), calls=%async_computation.13 | async-start | bytes 18874368 | tf_op jit(solution)/shard_map/reduce_scatter | solution.py:169
  784.1 963.0 %reduce-scatter.20.cloned.1.call-start = ((), (), s32[]{:S(2)}) async-start(), calls=%async_computation.14 | async-start | bytes 18874368 | tf_op jit(solution)/shard_map/reduce_scatter | solution.py:170
  800.0 236.5 %copy-start.47 = (f32[2048]{0:T(1024)S(1)}, f32[2048]{0:T(1024)}, u32[]{:S(2)}) copy-start(f32[2048]{0:T(1024)} %get-tuple-element.71) | copy-start | bytes 24580
  1067.4 9.6 copy-start.4
  1067.4 679.7 %copy-start.1 = (bf16[512,2048]{1,0:T(8,128)(2,1)S(1)}, bf16[512,2048]{1,0:T(8,128)(2,1)}, u32[]{:S(2)}) copy-start(bf16[512,2048]{1,0:T(8,128)(2,1)} %param.30) | copy-start | bytes 6291460
  (9 other events, 8.7 us)
Sparse Core Ops, SparseCore 0:
  71.9 299.7 all-gather.2
  472.9 172.0 all-reduce.13
  722.6 308.0 all-reduce.15
  1033.4 51.4 reduce-scatter.11
  1087.6 48.4 reduce-scatter.13
  1138.8 48.3 reduce-scatter.9
  1190.1 48.3 reduce-scatter.7
  1241.5 166.6 reduce-scatter.15
  1411.1 166.6 reduce-scatter.17
  1580.5 166.6 reduce-scatter.19
